TPU v7x, 256 devices: a whole 4x4x8 slice. The times are simulated.
256 devices in a mesh: tm: 8 (over x, z_lo), space: 32 (over z_hi, y, core).
Axes of the slice: x: 4, y: 4, z: 8 (z_hi: 4, z_lo: 2; z = z_hi * 2 + z_lo), core: 2. Of those that a mesh axis runs over, the one named last changes fastest.
Arguments:
- panels_in: float32 [32, 16384], P(None, 'space'), may hold values from -120 to 120
- blocks: float32 [16, 256, 3, 4096], P('tm', 'space'), may hold values from -0.4375 to 0.4375
- block_mask: int32 [16, 256, 3], P('tm', 'space'), may hold values 0 or 1
- mixing: float32 [16, 4, 8, 8], P('tm'), may hold values from -0.6 to 0.6
Outputs:
- forward_states: float32 [8, 32, 16384], P('tm', None, 'space')
- adjoint_states: float32 [8, 32, 16384], P('tm', None, 'space')
All inputs are finite; a program needn't handle non-finite values. No bound on the sum of `block_mask` on one device may be relied on, other than what follows from the above.
Results may differ from a plain program's by a relative error of at most 0.0003.
Values sent between devices are 32-bit elements; how exact they have to be, the bound alone decides.
A program may use at most 64 MiB of HBM per device.

v0:
```python
import jax
import jax.numpy as jnp
from jax import lax
from jax.sharding import PartitionSpec as P

BLOCK = 64
COLS = 8
PANELS = 4
TRANSFER_RUN = 2


def extended_2(block, sides, width):
    for axis, dim in sides:
        count = lax.axis_size(axis)
        forward = [(i, i + 1) for i in range(count - 1)]
        backward = [(target, source) for source, target in forward]
        low = lax.ppermute(
            lax.slice_in_dim(block, block.shape[dim] - width, None, axis=dim), axis, forward
        )
        high = lax.ppermute(lax.slice_in_dim(block, 0, width, axis=dim), axis, backward)
        block = jnp.concatenate([low, block, high], axis=dim)
    return block


def shifted(block, axis, distance):
    devices = range(lax.axis_size(axis))
    route = [(i - distance, i) for i in devices if i - distance in devices]
    return lax.ppermute(block, axis, route)


def push_step(blocks_here, working):
    count_cols = working.shape[0]
    count_blocks = blocks_here.shape[0]
    reshaped_block = working.reshape(count_cols, count_blocks, BLOCK)
    padded = jnp.pad(reshaped_block, ((0, 0), (1, 1), (0, 0)))
    pieces = jnp.stack(
        [
            padded[:, 0:count_blocks],
            padded[:, 1 : count_blocks + 1],
            padded[:, 2 : count_blocks + 2],
        ],
        axis=2,
    )
    matrices = blocks_here.reshape(count_blocks, 3, BLOCK, BLOCK)
    result = jnp.einsum("bjik,cbjk->cbi", matrices, pieces, precision=lax.Precision.HIGHEST)
    return result.reshape(count_cols, count_blocks * BLOCK)


def pull_step(blocks_here, working):
    count_cols = working.shape[0]
    count_blocks = blocks_here.shape[0]
    reshaped_block = working.reshape(count_cols, count_blocks, BLOCK)
    matrices = blocks_here.reshape(count_blocks, 3, BLOCK, BLOCK)
    products = jnp.einsum(
        "bjik,cbi->cbjk", matrices, reshaped_block, precision=lax.Precision.HIGHEST
    )
    first_part = products[:, :, 0]
    middle_part = products[:, :, 1]
    last_part = products[:, :, 2]
    result = (
        middle_part
        + jnp.pad(first_part[:, 1:], ((0, 0), (0, 1), (0, 0)))
        + jnp.pad(last_part[:, :-1], ((0, 0), (1, 0), (0, 0)))
    )
    return result.reshape(count_cols, count_blocks * BLOCK)


def mix_columns(working, expansion_weights):
    panel_count = expansion_weights.shape[0]
    reshaped_block = working.reshape(panel_count, COLS, working.shape[1])
    blended_panel = jnp.einsum(
        "yit,yif->ytf", expansion_weights, reshaped_block, precision=lax.Precision.HIGHEST
    )
    return working - blended_panel.reshape(working.shape)


def rescale(current):
    own_sums = jnp.sum(current * current, axis=1)
    all_sums = lax.psum(own_sums, "space")
    box_total = current.shape[1] * lax.axis_size("space")
    return current / jnp.sqrt(all_sums / box_total + 1e-06)[:, None]


def owner_pair(current, expansion_weights, extended, forward):
    box_count = current.shape[1]
    margin = TRANSFER_RUN * BLOCK
    if forward:
        step_order = list(range(TRANSFER_RUN))
        apply_step = push_step
    else:
        step_order = list(range(TRANSFER_RUN - 1, -1, -1))
        apply_step = pull_step
    for step_index in step_order:
        working = extended_2(current, (("space", 1),), BLOCK)
        working = jnp.pad(working, ((0, 0), (margin - BLOCK, margin - BLOCK)))
        working = mix_columns(
            apply_step(extended[step_index], working), expansion_weights[step_index]
        )
        current = working[:, margin : margin + box_count]
    return rescale(current)


def sweep(source, mixing, extended, forward, columns_pass):
    owning_devices = lax.axis_size("tm")
    own_index = lax.axis_index("tm")
    if forward:
        position = own_index
    else:
        position = owning_devices - 1 - own_index
    passes = source.shape[0] // columns_pass

    def one_section(section_index, carry):
        incoming, stored = carry
        panel_index = section_index - position
        current = jnp.where(position == 0, source, incoming)
        result = owner_pair(current, mixing, extended, forward)
        in_range = (panel_index >= 0) & (panel_index < passes)
        stored = jnp.where(in_range, result, stored)
        if forward:
            incoming = shifted(result, "tm", 1)
        else:
            incoming = shifted(result, "tm", -1)
        return (incoming, stored)

    start_carry = (jnp.zeros((columns_pass, source.shape[1]), jnp.float32), jnp.zeros_like(source))
    return lax.fori_loop(0, passes + owning_devices - 1, one_section, start_carry)[1]


def shards(panels_in, blocks, block_mask, mixing):
    masked = blocks * block_mask.astype(jnp.float32)[:, :, :, None]
    rim_blocks = jnp.concatenate([masked[:, :TRANSFER_RUN], masked[:, -TRANSFER_RUN:]], axis=1)
    received = extended_2(rim_blocks, (("space", 1),), TRANSFER_RUN)
    extended = jnp.concatenate(
        [received[:, :TRANSFER_RUN], masked, received[:, 3 * TRANSFER_RUN :]], axis=1
    )
    columns_pass = PANELS * COLS
    forward_store = sweep(panels_in, mixing, extended, True, columns_pass)
    adjoint_store = sweep(forward_store, mixing, extended, False, columns_pass)
    return (forward_store[None], adjoint_store[None])


def solution(mesh):
    return jax.shard_map(
        shards,
        mesh=mesh,
        in_specs=(
            P(None, "space"),
            P("tm", "space", None, None),
            P("tm", "space", None),
            P("tm", None, None, None),
        ),
        out_specs=(P("tm", None, "space"), P("tm", None, "space")),
        check_vma=False,
    )
```

profile of v0, /device:TPU:162, one launch (start us, length us, event | category | flops | bytes accessed | tf_op | source)
XLA Modules:
  0.0 1835.0 jit_solution(12119634927245568571)
XLA Ops:
  2.7 4.4 collective-permute-start.11
  10.8 9.4 collective-permute-done.10
  20.5 917.5 %while.36 = (s32[]{:T(128)}, f32[32,512]{1,0:T(8,128)S(1)}, f32[32,512]{1,0:T(8,128)}, pred[]{:T(512)}, f32[32,512]{1,0:T(8,128)S(1)}, /*index=5*/f32[2,12,3,409...) while((s32[]{:T(128)}, f32[32,512]{1,0:T(8,128)S(1)}, ...), condition=%wide.region_3.4_spmd.clone, body=%wide.region_0.3_spmd.clone.sunk | while | flops 118808648 | bytes 14009666 | solution.py:126
  28.2 4.5 collective-permute-done.1
  48.7 6.3 collective-permute-done.3
  58.3 69.9 %psum.32 = f32[32]{0:T(128)S(1)} all-reduce(f32[32]{0:T(128)S(1)} %multiply_reduce_fusion.4), channel_id=1, replica_groups=mesh['tm'=8,'space'=32] {'space'}, use_global_device_ids=true, to_apply=%region_2.2 | all-reduce | flops 32 | bytes 256 | tf_op jit(solution)/shard_map/while/body/eval_jaxpr/psum | solution.py:79
  142.2 4.5 collective-permute-done.1
  162.7 6.3 collective-permute-done.3
  172.3 69.9 %psum.32 = f32[32]{0:T(128)S(1)} all-reduce(f32[32]{0:T(128)S(1)} %multiply_reduce_fusion.4), channel_id=1, replica_groups=mesh['tm'=8,'space'=32] {'space'}, use_global_device_ids=true, to_apply=%region_2.2 | all-reduce | flops 32 | bytes 256 | tf_op jit(solution)/shard_map/while/body/eval_jaxpr/psum | solution.py:79
  256.1 4.5 collective-permute-done.1
  276.6 6.3 collective-permute-done.3
  286.3 69.9 %psum.32 = f32[32]{0:T(128)S(1)} all-reduce(f32[32]{0:T(128)S(1)} %multiply_reduce_fusion.4), channel_id=1, replica_groups=mesh['tm'=8,'space'=32] {'space'}, use_global_device_ids=true, to_apply=%region_2.2 | all-reduce | flops 32 | bytes 256 | tf_op jit(solution)/shard_map/while/body/eval_jaxpr/psum | solution.py:79
  356.3 5.1 collective-permute-start.4
  370.9 4.5 collective-permute-done.1
  391.4 6.3 collective-permute-done.3
  401.1 69.9 %psum.32 = f32[32]{0:T(128)S(1)} all-reduce(f32[32]{0:T(128)S(1)} %multiply_reduce_fusion.4), channel_id=1, replica_groups=mesh['tm'=8,'space'=32] {'space'}, use_global_device_ids=true, to_apply=%region_2.2 | all-reduce | flops 32 | bytes 256 | tf_op jit(solution)/shard_map/while/body/eval_jaxpr/psum | solution.py:79
  471.1 5.2 collective-permute-start.4
  485.9 4.5 collective-permute-done.1
  506.4 6.3 collective-permute-done.3
  516.0 69.9 %psum.32 = f32[32]{0:T(128)S(1)} all-reduce(f32[32]{0:T(128)S(1)} %multiply_reduce_fusion.4), channel_id=1, replica_groups=mesh['tm'=8,'space'=32] {'space'}, use_global_device_ids=true, to_apply=%region_2.2 | all-reduce | flops 32 | bytes 256 | tf_op jit(solution)/shard_map/while/body/eval_jaxpr/psum | solution.py:79
  586.1 5.2 collective-permute-start.4
  600.8 4.5 collective-permute-done.1
  621.3 6.3 collective-permute-done.3
  631.0 69.9 %psum.32 = f32[32]{0:T(128)S(1)} all-reduce(f32[32]{0:T(128)S(1)} %multiply_reduce_fusion.4), channel_id=1, replica_groups=mesh['tm'=8,'space'=32] {'space'}, use_global_device_ids=true, to_apply=%region_2.2 | all-reduce | flops 32 | bytes 256 | tf_op jit(solution)/shard_map/while/body/eval_jaxpr/psum | solution.py:79
  701.0 5.2 collective-permute-start.4
  715.8 4.5 collective-permute-done.1
  736.3 6.3 collective-permute-done.3
  745.9 69.9 %psum.32 = f32[32]{0:T(128)S(1)} all-reduce(f32[32]{0:T(128)S(1)} %multiply_reduce_fusion.4), channel_id=1, replica_groups=mesh['tm'=8,'space'=32] {'space'}, use_global_device_ids=true, to_apply=%region_2.2 | all-reduce | flops 32 | bytes 256 | tf_op jit(solution)/shard_map/while/body/eval_jaxpr/psum | solution.py:79
  816.0 5.2 collective-permute-start.4
  830.7 4.5 collective-permute-done.1
  851.2 6.3 collective-permute-done.3
  860.9 69.9 %psum.32 = f32[32]{0:T(128)S(1)} all-reduce(f32[32]{0:T(128)S(1)} %multiply_reduce_fusion.4), channel_id=1, replica_groups=mesh['tm'=8,'space'=32] {'space'}, use_global_device_ids=true, to_apply=%region_2.2 | all-reduce | flops 32 | bytes 256 | tf_op jit(solution)/shard_map/while/body/eval_jaxpr/psum | solution.py:79
  930.9 5.2 collective-permute-start.4
  938.0 897.0 %while.37 = (s32[]{:T(128)}, f32[32,512]{1,0:T(8,128)S(1)}, f32[32,512]{1,0:T(8,128)}, pred[]{:T(512)}, f32[32,512]{1,0:T(8,128)}, /*index=5*/f32[2,12,3,4096]{3...) while((s32[]{:T(128)}, f32[32,512]{1,0:T(8,128)S(1)}, ...), condition=%wide.region_7.8_spmd.clone, body=%wide.region_4.7_spmd.clone.sunk | while | flops 118612040 | bytes 13845762 | solution.py:126
  945.7 4.5 collective-permute-done.6
  963.8 6.3 collective-permute-done.8
  973.1 69.9 %psum.33 = f32[32]{0:T(128)S(1)} all-reduce(f32[32]{0:T(128)S(1)} %multiply_reduce_fusion.5), channel_id=1, replica_groups=mesh['tm'=8,'space'=32] {'space'}, use_global_device_ids=true, to_apply=%region_6.6 | all-reduce | flops 32 | bytes 256 | tf_op jit(solution)/shard_map/while/body/eval_jaxpr/psum | solution.py:79
  1058.2 4.5 collective-permute-done.6
  1076.3 6.3 collective-permute-done.8
  1085.6 69.9 %psum.33 = f32[32]{0:T(128)S(1)} all-reduce(f32[32]{0:T(128)S(1)} %multiply_reduce_fusion.5), channel_id=1, replica_groups=mesh['tm'=8,'space'=32] {'space'}, use_global_device_ids=true, to_apply=%region_6.6 | all-reduce | flops 32 | bytes 256 | tf_op jit(solution)/shard_map/while/body/eval_jaxpr/psum | solution.py:79
  1170.3 4.5 collective-permute-done.6
  1188.4 6.3 collective-permute-done.8
  1197.6 69.9 %psum.33 = f32[32]{0:T(128)S(1)} all-reduce(f32[32]{0:T(128)S(1)} %multiply_reduce_fusion.5), channel_id=1, replica_groups=mesh['tm'=8,'space'=32] {'space'}, use_global_device_ids=true, to_apply=%region_6.6 | all-reduce | flops 32 | bytes 256 | tf_op jit(solution)/shard_map/while/body/eval_jaxpr/psum | solution.py:79
  1270.1 4.6 collective-permute-done.9
  1282.4 4.7 collective-permute-done.6
  1300.4 6.3 collective-permute-done.8
  1309.7 69.9 %psum.33 = f32[32]{0:T(128)S(1)} all-reduce(f32[32]{0:T(128)S(1)} %multiply_reduce_fusion.5), channel_id=1, replica_groups=mesh['tm'=8,'space'=32] {'space'}, use_global_device_ids=true, to_apply=%region_6.6 | all-reduce | flops 32 | bytes 256 | tf_op jit(solution)/shard_map/while/body/eval_jaxpr/psum | solution.py:79
  1381.6 5.1 collective-permute-done.9
  1394.4 4.7 collective-permute-done.6
  1412.5 6.3 collective-permute-done.8
  1421.8 69.9 %psum.33 = f32[32]{0:T(128)S(1)} all-reduce(f32[32]{0:T(128)S(1)} %multiply_reduce_fusion.5), channel_id=1, replica_groups=mesh['tm'=8,'space'=32] {'space'}, use_global_device_ids=true, to_apply=%region_6.6 | all-reduce | flops 32 | bytes 256 | tf_op jit(solution)/shard_map/while/body/eval_jaxpr/psum | solution.py:79
  1493.7 5.1 collective-permute-done.9
  1506.5 4.7 collective-permute-done.6
  1524.6 6.3 collective-permute-done.8
  1533.8 69.9 %psum.33 = f32[32]{0:T(128)S(1)} all-reduce(f32[32]{0:T(128)S(1)} %multiply_reduce_fusion.5), channel_id=1, replica_groups=mesh['tm'=8,'space'=32] {'space'}, use_global_device_ids=true, to_apply=%region_6.6 | all-reduce | flops 32 | bytes 256 | tf_op jit(solution)/shard_map/while/body/eval_jaxpr/psum | solution.py:79
  1605.8 5.1 collective-permute-done.9
  1618.5 4.7 collective-permute-done.6
  1636.6 6.3 collective-permute-done.8
  1645.9 69.9 %psum.33 = f32[32]{0:T(128)S(1)} all-reduce(f32[32]{0:T(128)S(1)} %multiply_reduce_fusion.5), channel_id=1, replica_groups=mesh['tm'=8,'space'=32] {'space'}, use_global_device_ids=true, to_apply=%region_6.6 | all-reduce | flops 32 | bytes 256 | tf_op jit(solution)/shard_map/while/body/eval_jaxpr/psum | solution.py:79
  1717.8 5.1 collective-permute-done.9
  1730.6 4.7 collective-permute-done.6
  1748.7 6.3 collective-permute-done.8
  1758.0 69.9 %psum.33 = f32[32]{0:T(128)S(1)} all-reduce(f32[32]{0:T(128)S(1)} %multiply_reduce_fusion.5), channel_id=1, replica_groups=mesh['tm'=8,'space'=32] {'space'}, use_global_device_ids=true, to_apply=%region_6.6 | all-reduce | flops 32 | bytes 256 | tf_op jit(solution)/shard_map/while/body/eval_jaxpr/psum | solution.py:79
  1829.9 5.1 collective-permute-done.9
  (868 shorter events, 462.0 us)
Async XLA Ops:
  2.7 8.1 collective-permute-start.11
  7.1 13.1 collective-permute-start.10
  21.2 7.0 collective-permute-start
  23.1 9.6 collective-permute-start.1
  45.4 9.6 collective-permute-start.3
  135.2 7.0 collective-permute-start
  137.1 9.6 collective-permute-start.1
  159.4 9.6 collective-permute-start.3
  249.2 7.0 collective-permute-start
  251.1 9.6 collective-permute-start.1
  273.4 9.6 collective-permute-start.3
  356.3 7.0 collective-permute-start.4
  364.0 7.0 collective-permute-start
  365.9 9.6 collective-permute-start.1
  388.2 9.6 collective-permute-start.3
  471.1 7.1 collective-permute-start.4
  478.9 7.0 collective-permute-start
  480.8 9.6 collective-permute-start.1
  503.1 9.6 collective-permute-start.3
  586.1 7.1 collective-permute-start.4
  593.9 7.0 collective-permute-start
  595.8 9.6 collective-permute-start.1
  618.1 9.6 collective-permute-start.3
  701.0 7.1 collective-permute-start.4
  708.8 7.0 collective-permute-start
  710.7 9.6 collective-permute-start.1
  733.0 9.6 collective-permute-start.3
  816.0 7.1 collective-permute-start.4
  823.8 7.0 collective-permute-start
  825.7 9.6 collective-permute-start.1
  848.0 9.6 collective-permute-start.3
  930.9 7.1 collective-permute-start.4
  938.8 7.0 collective-permute-start.5
  940.7 9.6 collective-permute-start.6
  960.5 9.6 collective-permute-start.8
  1043.1 7.4 collective-permute-start.9
  1051.3 7.0 collective-permute-start.5
  1053.2 9.6 collective-permute-start.6
  1073.0 9.6 collective-permute-start.8
  1155.6 7.1 collective-permute-start.9
  1163.3 7.0 collective-permute-start.5
  1165.2 9.6 collective-permute-start.6
  1185.1 9.6 collective-permute-start.8
  1267.6 7.1 collective-permute-start.9
  1275.4 7.0 collective-permute-start.5
  1277.3 9.7 collective-permute-start.6
  1297.2 9.6 collective-permute-start.8
  1379.7 7.1 collective-permute-start.9
  1387.5 7.0 collective-permute-start.5
  1389.4 9.7 collective-permute-start.6
  1409.2 9.6 collective-permute-start.8
  1491.8 7.1 collective-permute-start.9
  1499.5 7.0 collective-permute-start.5
  1501.4 9.7 collective-permute-start.6
  1521.3 9.6 collective-permute-start.8
  1603.8 7.1 collective-permute-start.9
  1611.6 7.0 collective-permute-start.5
  1613.5 9.7 collective-permute-start.6
  1633.4 9.6 collective-permute-start.8
  1715.9 7.1 collective-permute-start.9
  1723.6 7.0 collective-permute-start.5
  1725.6 9.7 collective-permute-start.6
  1745.4 9.6 collective-permute-start.8
  1827.9 7.1 collective-permute-start.9
  (132 other events, 2125.1 us)
where the time goes:
time: 1840 us
  blocking collectives  1120 us (61%)
  waiting for transfers between devices  239 us (13%)
  starting transfers between devices  209 us (11%)
  local copies, waits for them, and re-layouts  169 us (9%)
  matrix products  51.1 us (3%)
  other arithmetic  44.3 us (2%)
    psum x16, blocking collectives, rescale(): all_sums = lax.psum(own_sums, 'space')  1120 us
    ppermute x33, waiting for transfers between devices, extended_2(): lax.ppermute(lax.slice_in_dim(block, block.shape[dim] - width, None, axis...  184 us
    ppermute x33, starting transfers between devices, extended_2(): lax.ppermute(lax.slice_in_dim(block, 0, width, axis=dim), axis, backward)  79.6 us
    ppermute x33, starting transfers between devices, extended_2(): lax.ppermute(lax.slice_in_dim(block, block.shape[dim] - width, None, axis...  71.2 us
    ppermute x16, starting transfers between devices, shifted(): return lax.ppermute(block, axis, route)  57.8 us
    ppermute x16, waiting for transfers between devices, shifted(): return lax.ppermute(block, axis, route)  53.7 us
    concatenate x32, other arithmetic, extended_2(): block = jnp.concatenate([low, block, high], axis=dim)  37.7 us
  transfers between devices with their start and end apart: 82, of which 50 were waited for; matrix products, arithmetic and copies ran while one was open for 3% of the time, Pallas kernels for 0%

commit v1 on v0

v1 whole, which is shorter than its diff:
```python
import functools

import jax
import jax.numpy as jnp
from jax import lax
from jax.experimental import pallas as pl
from jax.experimental.pallas import tpu as pltpu
from jax.sharding import PartitionSpec as P

BLOCK = 64
COLS = 8
PANELS = 4
ROWS = PANELS * COLS
TILE_BLOCKS = 8
TILE = TILE_BLOCKS * BLOCK
EDGE = 2 * BLOCK
LAG = 3
MESH = pl.DeviceIdType.MESH
F32 = jnp.float32
BF16 = jnp.bfloat16
HIGHEST = lax.Precision.HIGHEST


def halves(value):
    high = value.astype(BF16)
    low = (value - high.astype(F32)).astype(BF16)
    return high, low


def dot(a, b):
    return jnp.dot(a, b, preferred_element_type=F32)


def dot_exact(a, b):
    return jnp.dot(a, b, precision=HIGHEST, preferred_element_type=F32)


def dot_exact_nt(a, b):
    return lax.dot_general(
        a, b, (((1,), (1,)), ((), ())), precision=HIGHEST, preferred_element_type=F32
    )


def product(value, high, low):
    rows = value.shape[0]
    value_high, value_low = halves(value)
    both = dot(jnp.concatenate([value_high, value_low], axis=0), high)
    return both[:rows] + both[rows:] + dot(value_high, low)


def kernel(
    n_tm,
    n_space,
    near,
    panels_hbm,
    blocks_hbm,
    mask_ref,
    mixing_ref,
    forward_hbm,
    adjoint_hbm,
    raw,
    first,
    second,
    edge_low,
    edge_high,
    halo_low,
    halo_high,
    step_high,
    step_low,
    turned_high,
    turned_low,
    mix_forward,
    mix_adjoint,
    wide,
    state,
    spread,
    back,
    back_low,
    back_high,
    own_low,
    own_high,
    adjoint_state,
    gram_near,
    gram_far,
    chain_in,
    chain_out,
    scale_in,
    scale_out,
    result,
    local_sem,
    halo_send,
    halo_recv,
    wide_send,
    wide_recv,
    back_send,
    back_recv,
    own_send,
    own_recv,
    near_send,
    near_recv,
    far_send,
    far_recv,
    chain_send,
    chain_recv,
    scale_send,
    scale_recv,
):
    a = lax.axis_index("tm")
    s = lax.axis_index("space")
    far = n_space // near
    top = n_tm - 1
    near_base = (s // near) * near
    near_own = s % near
    far_own = s // near
    box_total = n_space * TILE
    has_left = s > 0
    has_right = s < n_space - 1

    barrier = pltpu.get_barrier_semaphore()

    def greet(condition, row, tile):
        @pl.when(condition)
        def _():
            pl.semaphore_signal(barrier, inc=1, device_id=(row, tile), device_id_type=MESH)

        return jnp.where(condition, 1, 0)

    greeted = jnp.int32(near - 1 + far - 1)
    for offset in range(1, near):
        tile = near_base + lax.rem(near_own + offset, near)
        pl.semaphore_signal(barrier, inc=1, device_id=(a, tile), device_id_type=MESH)
    for offset in range(1, far):
        tile = near_own + near * lax.rem(far_own + offset, far)
        pl.semaphore_signal(barrier, inc=1, device_id=(a, tile), device_id_type=MESH)
    for row_step in (-1, 0, 1):
        for tile_step in (-1, 0, 1):
            if row_step == 0 and tile_step == 0:
                continue
            row, tile = a + row_step, s + tile_step
            inside = (row >= 0) & (row <= top) & (tile >= 0) & (tile < n_space)
            greeted = greeted + greet(inside, row, tile)
    for condition, row in (
        (a <= top - LAG, a + LAG),
        (a >= LAG, a - LAG),
        (a == top - 2, a + 2),
        (a == top, a - 2),
    ):
        greeted = greeted + greet(condition, row, s)

    copy_blocks = pltpu.make_async_copy(blocks_hbm, raw, local_sem.at[0])
    copy_blocks.start()
    copy_panels = pltpu.make_async_copy(
        panels_hbm, wide.at[:, pl.ds(EDGE, TILE)], local_sem.at[1]
    )

    @pl.when(a == 0)
    def _():
        copy_panels.start()

    first[...] = jnp.zeros_like(first)
    second[...] = jnp.zeros_like(second)

    @pl.when(s == 0)
    def _():
        wide[:, 0:EDGE] = jnp.zeros((ROWS, EDGE), F32)
        halo_low[...] = jnp.zeros_like(halo_low)

    @pl.when(s == n_space - 1)
    def _():
        wide[:, EDGE + TILE : 2 * EDGE + TILE] = jnp.zeros((ROWS, EDGE), F32)
        halo_high[...] = jnp.zeros_like(halo_high)

    lane = lax.broadcasted_iota(jnp.int32, (32, 128), 1)
    is_left = lane < BLOCK

    def pair(left, right):
        if left is None:
            even = jnp.where(is_left, 0.0, pltpu.roll(right, BLOCK, 1))
            odd = jnp.where(is_left, 0.0, right)
        elif right is None:
            even = jnp.where(is_left, left, 0.0)
            odd = jnp.where(is_left, pltpu.roll(left, BLOCK, 1), 0.0)
        else:
            even = jnp.where(is_left, left, pltpu.roll(right, BLOCK, 1))
            odd = jnp.where(is_left, pltpu.roll(left, BLOCK, 1), right)
        return even, odd

    def put(target, row, values):
        for parity in range(2):
            target[pl.ds(row + parity, 32, stride=2), :] = values[parity]

    def lanes(ref, start, stop, row, rows):
        tiles = [ref[tile, row : row + rows, :] for tile in range(start, stop)]
        return jnp.concatenate(tiles, axis=1)

    copy_blocks.wait()
    for step in range(2):
        for block in range(TILE_BLOCKS):
            packed = []
            for j in range(3):
                start = (step * 3 + j) * 256 + block
                scale = mask_ref[step * 24 + block * 3 + j].astype(F32)
                packed.append(raw[pl.ds(start, 32, stride=8), :] * scale)
            if block % 2 == 0:
                tiles = [(None, packed[0]), (packed[1], packed[2])]
                tile_index = block // 2 - 1
            else:
                tiles = [(packed[0], packed[1]), (packed[2], None)]
                tile_index = (block - 1) // 2
            for extra in range(2):
                values = pair(*tiles[extra])
                index = tile_index + extra
                if step == 0:
                    put(first.at[index + 1], block * BLOCK, values)
                elif index < 0:
                    put(edge_low, 0, values)
                elif index >= TILE // 128:
                    put(edge_high, 0, values)
                else:
                    put(second.at[index], block * BLOCK, values)

    pl.semaphore_wait(barrier, greeted)

    send_right = pltpu.make_async_remote_copy(
        src_ref=first.at[pl.ds(4, 2), pl.ds(TILE - BLOCK, BLOCK)],
        dst_ref=halo_low,
        send_sem=halo_send.at[0],
        recv_sem=halo_recv.at[0],
        device_id=(a, s + 1),
        device_id_type=MESH,
    )
    send_left = pltpu.make_async_remote_copy(
        src_ref=first.at[pl.ds(0, 2), pl.ds(0, BLOCK)],
        dst_ref=halo_high,
        send_sem=halo_send.at[1],
        recv_sem=halo_recv.at[1],
        device_id=(a, s - 1),
        device_id_type=MESH,
    )

    def copies_wide(source, row, base):
        center = pltpu.make_async_remote_copy(
            src_ref=source,
            dst_ref=wide.at[:, pl.ds(EDGE, TILE)],
            send_sem=wide_send.at[base],
            recv_sem=wide_recv.at[0],
            device_id=(row, s),
            device_id_type=MESH,
        )
        right = pltpu.make_async_remote_copy(
            src_ref=source.at[:, pl.ds(TILE - EDGE, EDGE)],
            dst_ref=wide.at[:, pl.ds(0, EDGE)],
            send_sem=wide_send.at[base + 1],
            recv_sem=wide_recv.at[1],
            device_id=(row, s + 1),
            device_id_type=MESH,
        )
        left = pltpu.make_async_remote_copy(
            src_ref=source.at[:, pl.ds(0, EDGE)],
            dst_ref=wide.at[:, pl.ds(EDGE + TILE, EDGE)],
            send_sem=wide_send.at[base + 2],
            recv_sem=wide_recv.at[2],
            device_id=(row, s - 1),
            device_id_type=MESH,
        )
        return center, right, left

    _, panel_right, panel_left = copies_wide(panels_hbm, a, 0)
    state_center, state_right, state_left = copies_wide(state, a + 1, 3)

    @pl.when((a == 0) & has_right)
    def _():
        panel_right.start()

    @pl.when((a == 0) & has_left)
    def _():
        panel_left.start()

    @pl.when(has_right)
    def _():
        send_right.start()

    @pl.when(has_left)
    def _():
        send_left.start()

    def formed(group):
        mid = 128 * group
        left = lanes(second, group, group + 3, 256 * group, 256)
        right = lanes(first, 2 * group, 2 * group + 4, mid, 384)
        right_high, right_low = halves(right)
        return product(left, right_high, right_low)

    group_low = formed(0)
    group_high = formed(1)

    row_index = lax.broadcasted_iota(jnp.int32, (ROWS, ROWS), 0)
    col_index = lax.broadcasted_iota(jnp.int32, (ROWS, ROWS), 1)
    same_panel = row_index // COLS == col_index // COLS
    eye = jnp.where(row_index == col_index, 1.0, 0.0).astype(F32)
    spread_rows = lax.broadcasted_iota(jnp.int32, (COLS, ROWS), 0)
    spread_cols = lax.broadcasted_iota(jnp.int32, (COLS, ROWS), 1)
    repeat = jnp.where(spread_cols % COLS == spread_rows, 1.0, 0.0).astype(F32)

    def mixer(step):
        stacked = jnp.concatenate([mixing_ref[step, p] for p in range(PANELS)], axis=0)
        return eye - jnp.where(same_panel, dot_exact(stacked, repeat), 0.0)

    mixer_first = mixer(0)
    mixer_second = mixer(1)
    mix_forward[...] = dot_exact_nt(eye, dot_exact(mixer_first, mixer_second))
    mix_adjoint[...] = dot_exact_nt(eye, dot_exact(mixer_second, mixer_first))

    @pl.when(has_left)
    def _():
        send_right.wait_recv()

    @pl.when(has_right)
    def _():
        send_left.wait_recv()

    beside_high, beside_low = halves(lanes(halo_low, 0, 2, 0, BLOCK))
    add_low = product(pltpu.roll(edge_low[...], BLOCK, 1)[:, :BLOCK], beside_high, beside_low)
    beside_high, beside_low = halves(lanes(halo_high, 0, 2, 0, BLOCK))
    add_high = product(edge_high[...][:, :BLOCK], beside_high, beside_low)
    group_low = jnp.concatenate(
        [
            jnp.concatenate([group_low[:BLOCK, :256] + add_low, group_low[:BLOCK, 256:]], axis=1),
            group_low[BLOCK:],
        ],
        axis=0,
    )
    group_high = jnp.concatenate(
        [
            group_high[: 256 - BLOCK],
            jnp.concatenate(
                [group_high[256 - BLOCK :, :256], group_high[256 - BLOCK :, 256:] + add_high],
                axis=1,
            ),
        ],
        axis=0,
    )
    for group, value in enumerate((group_low, group_high)):
        turned = jnp.transpose(value)
        turned_high[group], turned_low[group] = halves(turned)
        step_high[group], step_low[group] = halves(value)

    adjoint_center = pltpu.make_async_remote_copy(
        src_ref=spread.at[:, pl.ds(EDGE, TILE)],
        dst_ref=back,
        send_sem=back_send.at[0],
        recv_sem=back_recv.at[0],
        device_id=(a - 1, s),
        device_id_type=MESH,
    )

    def copies_edge(row, into_low, into_high, send_sems, recv_sems, base):
        right = pltpu.make_async_remote_copy(
            src_ref=spread.at[:, pl.ds(EDGE + TILE, EDGE)],
            dst_ref=into_low,
            send_sem=send_sems.at[base],
            recv_sem=recv_sems.at[base],
            device_id=(row, s + 1),
            device_id_type=MESH,
        )
        left = pltpu.make_async_remote_copy(
            src_ref=spread.at[:, pl.ds(0, EDGE)],
            dst_ref=into_high,
            send_sem=send_sems.at[base + 1],
            recv_sem=recv_sems.at[base + 1],
            device_id=(row, s - 1),
            device_id_type=MESH,
        )
        return right, left

    adjoint_right, adjoint_left = copies_edge(a - 1, back_low, back_high, back_send, back_recv, 1)
    own_right, own_left = copies_edge(a, own_low, own_high, own_send, own_recv, 0)

    def near_copy(pass_index, offset):
        tile = near_base + lax.rem(near_own + offset, near)
        return pltpu.make_async_remote_copy(
            src_ref=gram_near.at[pass_index, near_own],
            dst_ref=gram_near.at[pass_index, near_own],
            send_sem=near_send.at[pass_index, offset],
            recv_sem=near_recv.at[pass_index, near - offset],
            device_id=(a, tile),
            device_id_type=MESH,
        )

    def far_copy(pass_index, offset):
        tile = near_own + near * lax.rem(far_own + offset, far)
        return pltpu.make_async_remote_copy(
            src_ref=gram_far.at[pass_index, far_own],
            dst_ref=gram_far.at[pass_index, far_own],
            send_sem=far_send.at[pass_index, offset],
            recv_sem=far_recv.at[pass_index, far - offset],
            device_id=(a, tile),
            device_id_type=MESH,
        )

    def chain_copy(pass_index, target_pass, row):
        return pltpu.make_async_remote_copy(
            src_ref=chain_out.at[pass_index],
            dst_ref=chain_in.at[target_pass],
            send_sem=chain_send.at[pass_index],
            recv_sem=chain_recv.at[target_pass],
            device_id=(row, s),
            device_id_type=MESH,
        )

    def scale_copy(pass_index, target_pass, row):
        return pltpu.make_async_remote_copy(
            src_ref=scale_out.at[pass_index],
            dst_ref=scale_in.at[target_pass],
            send_sem=scale_send.at[pass_index],
            recv_sem=scale_recv.at[target_pass],
            device_id=(row, s),
            device_id_type=MESH,
        )

    def send_gram(pass_index, value):
        gram = dot_exact_nt(value, value)
        wide_gram = jnp.concatenate([gram, jnp.zeros((ROWS, 128 - ROWS), F32)], axis=1)
        rows_wide = lax.broadcasted_iota(jnp.int32, (ROWS, 128), 0)
        cols_wide = lax.broadcasted_iota(jnp.int32, (ROWS, 128), 1)
        kept = jnp.where(rows_wide // COLS == cols_wide // COLS, wide_gram, 0.0)
        compact = kept[0:COLS]
        for p in range(1, PANELS):
            compact = compact + kept[p * COLS : (p + 1) * COLS]
        gram_near[pass_index, near_own] = compact
        for offset in range(1, near):
            near_copy(pass_index, offset).start()

    def reduce_gram(pass_index):
        for offset in range(1, near):
            near_copy(pass_index, near - offset).wait_recv()
        total = gram_near[pass_index, 0]
        for slot in range(1, near):
            total = total + gram_near[pass_index, slot]
        gram_far[pass_index, far_own] = total
        for offset in range(1, far):
            far_copy(pass_index, offset).start()
        for offset in range(1, far):
            far_copy(pass_index, far - offset).wait_recv()
        total = gram_far[pass_index, 0]
        for slot in range(1, far):
            total = total + gram_far[pass_index, slot]
        return total

    def finish(pass_index, gram_sum, mix_ref, value_ref, out_copy):
        rows_wide = lax.broadcasted_iota(jnp.int32, (ROWS, 128), 0)
        cols_wide = lax.broadcasted_iota(jnp.int32, (ROWS, 128), 1)
        gram = jnp.where(
            rows_wide // COLS == cols_wide // COLS,
            jnp.concatenate([gram_sum] * PANELS, axis=0) / box_total,
            0.0,
        )
        size = jnp.sum(jnp.where(rows_wide == cols_wide, gram, 0.0)) / ROWS
        size = jnp.sqrt(jnp.full((8, 128), size, F32))
        before = chain_in[pass_index, 0:ROWS]
        size_before = chain_in[pass_index, ROWS : ROWS + 8]
        scale = scale_in[pass_index]
        mixed = dot_exact(mix_ref[...], before) / scale[0:1, :]
        squares = jnp.sum(dot_exact(mixed[:, :ROWS], gram) * mixed, axis=1, keepdims=True)
        combined = mixed / jnp.sqrt(jnp.maximum(squares, 0.0) + 1e-06)
        chain_out[pass_index, 0:ROWS] = combined
        chain_out[pass_index, ROWS : ROWS + 8] = size
        usable = (size > 1e-30) & (size_before > 1e-30)
        ratio = scale * (size_before / jnp.where(usable, size, 1.0))
        scale_out[pass_index] = jnp.where(usable, jnp.clip(ratio, 1e-12, 1e12), 1.0)
        return combined

    def emit(pass_index, combined, value_ref):
        result[pass_index] = dot_exact(combined[:, :ROWS], value_ref[...])

    out_forward = pltpu.make_async_copy(result.at[0], forward_hbm.at[0], local_sem.at[2])
    out_adjoint = pltpu.make_async_copy(result.at[1], adjoint_hbm.at[0], local_sem.at[3])

    lanes_eye = lax.broadcasted_iota(jnp.int32, (ROWS + 8, 128), 1)
    rows_eye = lax.broadcasted_iota(jnp.int32, (ROWS + 8, 128), 0)

    @pl.when(a == 0)
    def _():
        chain_in[0] = jnp.where((rows_eye == lanes_eye) | (rows_eye >= ROWS), 1.0, 0.0)
        copy_panels.wait()

    @pl.when(a < LAG)
    def _():
        scale_in[0] = jnp.ones((8, 128), F32)

    @pl.when(a >= LAG)
    def _():
        scale_copy(0, 0, a).wait_recv()

    @pl.when(a > 0)
    def _():
        state_center.wait_recv()

    @pl.when(has_left)
    def _():
        state_right.wait_recv()

    @pl.when(has_right)
    def _():
        state_left.wait_recv()

    for group in range(2):
        value = wide[:, 256 * group : 256 * group + 512]
        moved = product(value, turned_high[group], turned_low[group])
        state[:, 256 * group : 256 * group + 256] = moved * scale_in[0, 0:1, 0:1]

    @pl.when(a < top)
    def _():
        state_center.start()

    @pl.when((a < top) & has_right)
    def _():
        state_right.start()

    @pl.when((a < top) & has_left)
    def _():
        state_left.start()

    send_gram(0, state[...])

    def adjoint_apply(value):
        parts = []
        for group in range(2):
            parts.append(
                product(
                    value[:, 256 * group : 256 * group + 256], step_high[group], step_low[group]
                )
            )
        scale = scale_in[1, 0:1, 0:1]
        spread[:, 0:256] = parts[0][:, 0:256] * scale
        spread[:, 256:512] = (parts[0][:, 256:512] + parts[1][:, 0:256]) * scale
        spread[:, 512:768] = parts[1][:, 256:512] * scale

        @pl.when(a > 0)
        def _():
            adjoint_center.start()

        @pl.when((a > 0) & has_right)
        def _():
            adjoint_right.start()

        @pl.when((a > 0) & has_left)
        def _():
            adjoint_left.start()

        @pl.when(has_right)
        def _():
            own_right.start()

        @pl.when(has_left)
        def _():
            own_left.start()

        @pl.when(has_left)
        def _():
            own_right.wait_recv()

        @pl.when(has_right)
        def _():
            own_left.wait_recv()

        adjoint_state[...] = spread[:, EDGE : EDGE + TILE]

        @pl.when(has_left)
        def _():
            adjoint_state[:, 0:EDGE] = adjoint_state[:, 0:EDGE] + own_low[...]

        @pl.when(has_right)
        def _():
            adjoint_state[:, TILE - EDGE : TILE] = (
                adjoint_state[:, TILE - EDGE : TILE] + own_high[...]
            )

        send_gram(1, adjoint_state[...])

    @pl.when(a == top)
    def _():
        scale_copy(0, 1, a).wait_recv()
        adjoint_apply(state[...])

    forward_sum = reduce_gram(0)

    @pl.when(a > 0)
    def _():
        chain_copy(0, 0, a).wait_recv()

    forward_combined = finish(0, forward_sum, mix_forward, state, None)

    @pl.when(a < top)
    def _():
        chain_copy(0, 0, a + 1).start()

    @pl.when(a <= top - LAG)
    def _():
        scale_copy(0, 0, a + LAG).start()

    @pl.when(a == top - 2)
    def _():
        scale_copy(0, 1, a + 2).start()

    @pl.when(a == top)
    def _():
        scale_copy(0, 1, a - 2).start()
        chain_in[1] = chain_out[0]

    @pl.when(a == top - 1)
    def _():
        scale_in[1] = scale_out[0]

    emit(0, forward_combined, state)
    out_forward.start()

    @pl.when(a < top)
    def _():
        @pl.when(a != top - 1)
        def _():
            scale_copy(0, 1, a).wait_recv()

        adjoint_center.wait_recv()

        @pl.when(has_left)
        def _():
            adjoint_right.wait_recv()
            back[:, 0:EDGE] = back[:, 0:EDGE] + back_low[...]

        @pl.when(has_right)
        def _():
            adjoint_left.wait_recv()
            back[:, TILE - EDGE : TILE] = back[:, TILE - EDGE : TILE] + back_high[...]

        adjoint_apply(back[...])

    adjoint_sum = reduce_gram(1)

    @pl.when(a < top)
    def _():
        chain_copy(1, 1, a).wait_recv()

    adjoint_combined = finish(1, adjoint_sum, mix_adjoint, adjoint_state, None)

    @pl.when(a > 0)
    def _():
        chain_copy(1, 1, a - 1).start()

    @pl.when(a >= LAG)
    def _():
        scale_copy(1, 1, a - LAG).start()

    emit(1, adjoint_combined, adjoint_state)
    out_adjoint.start()

    @pl.when(has_right)
    def _():
        send_right.wait_send()
        own_right.wait_send()

    @pl.when(has_left)
    def _():
        send_left.wait_send()
        own_left.wait_send()

    @pl.when((a == 0) & has_right)
    def _():
        panel_right.wait_send()

    @pl.when((a == 0) & has_left)
    def _():
        panel_left.wait_send()

    @pl.when(a < top)
    def _():
        state_center.wait_send()
        chain_copy(0, 0, a + 1).wait_send()

    @pl.when((a < top) & has_right)
    def _():
        state_right.wait_send()

    @pl.when((a < top) & has_left)
    def _():
        state_left.wait_send()

    @pl.when(a > 0)
    def _():
        adjoint_center.wait_send()
        chain_copy(1, 1, a - 1).wait_send()

    @pl.when((a > 0) & has_right)
    def _():
        adjoint_right.wait_send()

    @pl.when((a > 0) & has_left)
    def _():
        adjoint_left.wait_send()

    @pl.when(a != top - 1)
    def _():
        scale_copy(0, 0, a).wait_send()

    @pl.when(a >= LAG)
    def _():
        scale_copy(1, 1, a).wait_send()

    for pass_index in range(2):
        for offset in range(1, near):
            near_copy(pass_index, offset).wait_send()
        for offset in range(1, far):
            far_copy(pass_index, offset).wait_send()
    out_forward.wait()
    out_adjoint.wait()


def solution(mesh):
    n_tm = mesh.shape["tm"]
    n_space = mesh.shape["space"]
    near = min(8, n_space) if n_space >= 8 else 2
    far = n_space // near

    def shards(panels_in, blocks, block_mask, mixing):
        lines = blocks.reshape(2, TILE_BLOCKS, 3, 32, 128).transpose(0, 2, 3, 1, 4)
        lines = lines.reshape(2 * 3 * 32 * TILE_BLOCKS, 128)
        dma = pltpu.SemaphoreType.DMA
        vmem = pltpu.VMEM
        scratch = [
            vmem((2 * 3 * 32 * TILE_BLOCKS, 128), F32),
            vmem((6, TILE, 128), F32),
            vmem((4, TILE, 128), F32),
            vmem((BLOCK, 128), F32),
            vmem((BLOCK, 128), F32),
            vmem((2, BLOCK, 128), F32),
            vmem((2, BLOCK, 128), F32),
            vmem((2, 256, 512), BF16),
            vmem((2, 256, 512), BF16),
            vmem((2, 512, 256), BF16),
            vmem((2, 512, 256), BF16),
            vmem((ROWS, ROWS), F32),
            vmem((ROWS, ROWS), F32),
            vmem((ROWS, TILE + 2 * EDGE), F32),
            vmem((ROWS, TILE), F32),
            vmem((ROWS, TILE + 2 * EDGE), F32),
            vmem((ROWS, TILE), F32),
            vmem((ROWS, EDGE), F32),
            vmem((ROWS, EDGE), F32),
            vmem((ROWS, EDGE), F32),
            vmem((ROWS, EDGE), F32),
            vmem((ROWS, TILE), F32),
            vmem((2, near, 8, 128), F32),
            vmem((2, far, 8, 128), F32),
            vmem((2, ROWS + 8, 128), F32),
            vmem((2, ROWS + 8, 128), F32),
            vmem((2, 8, 128), F32),
            vmem((2, 8, 128), F32),
            vmem((2, ROWS, TILE), F32),
            dma((4,)),
            dma((2,)),
            dma((2,)),
            dma((6,)),
            dma((3,)),
            dma((3,)),
            dma((3,)),
            dma((2,)),
            dma((2,)),
            dma((2, near)),
            dma((2, near)),
            dma((2, far)),
            dma((2, far)),
            dma((2,)),
            dma((2,)),
            dma((2,)),
            dma((2,)),
        ]
        shape = jax.ShapeDtypeStruct((1, ROWS, TILE), F32)
        return pl.pallas_call(
            functools.partial(kernel, n_tm, n_space, near),
            out_shape=(shape, shape),
            in_specs=[
                pl.BlockSpec(memory_space=pl.ANY),
                pl.BlockSpec(memory_space=pl.ANY),
                pl.BlockSpec(memory_space=pltpu.SMEM),
                pl.BlockSpec(memory_space=pltpu.VMEM),
            ],
            out_specs=(pl.BlockSpec(memory_space=pl.ANY), pl.BlockSpec(memory_space=pl.ANY)),
            scratch_shapes=scratch,
            compiler_params=pltpu.CompilerParams(collective_id=0, has_side_effects=True),
        )(panels_in, lines, block_mask.reshape(-1), mixing)

    return jax.shard_map(
        shards,
        mesh=mesh,
        in_specs=(
            P(None, "space"),
            P("tm", "space", None, None),
            P("tm", "space", None),
            P("tm", None, None, None),
        ),
        out_specs=(P("tm", None, "space"), P("tm", None, "space")),
        check_vma=False,
    )
```

time: 1840 us -> 120 us (0.07)
  the two profiles are of different devices: /device:TPU:162 before, /device:TPU:8 now
where the time goes in v1:
time: 120 us
  Pallas kernels  115 us (96%)
  local copies, waits for them, and re-layouts  3.51 us (3%)
    pallas_call x1, Pallas kernels, shards(): pl.pallas_call(functools.partial(kernel, n_tm, n_space, near), out_shape=...  115 us
    unnamed x5, local copies, waits for them, and re-layouts  2.9 us

profile of v1, /device:TPU:8, one launch (start us, length us, event | category | flops | bytes accessed | tf_op | source)
XLA Modules:
  0.0 119.5 jit_solution(802502512045273086)
XLA Ops:
  0.6 0.8 copy.7
  1.4 0.6 reshape.15.mask_ref
  2.0 115.4 %shard_map.59 = (f32[1,32,512]{2,1,0:T(8,128)}, f32[1,32,512]{2,1,0:T(8,128)}) custom-call(f32[32,512]{1,0:T(8,128)} %panels_hbm.1, f32[1536,128]{1,0:T(8,128)} %bitcast.5, s32[48]{0:T(128)} %reshape.15.mask_ref, f32[2,4,8,8]{3,2,1,0:T(8,128)} %mixing_ref.1), custom_call_target="tpu_custom_call" | custom-call | tf_op jit(solution)/shard_map/pallas_call | solution.py:778
  117.4 0.0 copy-start
  117.4 1.5 %copy.10 = f32[1,32,512]{2,1,0:T(8,128)} copy(f32[1,32,512]{2,1,0:T(8,128)} %get-tuple-element.4) | data formatting | bytes 131072
  118.9 0.0 copy-done
  118.9 0.6 copy.11
Async XLA Ops:
  117.4 1.5 %copy-start = (f32[1,32,512]{2,1,0:T(8,128)S(1)}, f32[1,32,512]{2,1,0:T(8,128)}, u32[]{:S(2)}) copy-start(f32[1,32,512]{2,1,0:T(8,128)} %get-tuple-element.5) | copy-start | bytes 196612

commit v2 on v0

v2 whole, which is shorter than its diff:
```python
import functools

import jax
import jax.numpy as jnp
from jax import lax
from jax.experimental import pallas as pl
from jax.experimental.pallas import tpu as pltpu
from jax.sharding import PartitionSpec as P

BLOCK = 64
COLS = 8
PANELS = 4
ROWS = PANELS * COLS
TILE_BLOCKS = 8
TILE = TILE_BLOCKS * BLOCK
EDGE = 2 * BLOCK
LAG = 4
STRIP = EDGE + 2 * EDGE
START = 2.0**-10
MESH = pl.DeviceIdType.MESH
F32 = jnp.float32
BF16 = jnp.bfloat16
HIGHEST = lax.Precision.HIGHEST


def halves(value):
    high = value.astype(BF16)
    low = (value - high.astype(F32)).astype(BF16)
    return high, low


def dot(a, b):
    return jnp.dot(a, b, preferred_element_type=F32)


def dot_exact(a, b):
    return jnp.dot(a, b, precision=HIGHEST, preferred_element_type=F32)


def dot_exact_nt(a, b):
    return lax.dot_general(
        a, b, (((1,), (1,)), ((), ())), precision=HIGHEST, preferred_element_type=F32
    )


def product(value, high, low):
    rows = value.shape[0]
    value_high, value_low = halves(value)
    both = dot(jnp.concatenate([value_high, value_low], axis=0), high)
    return both[:rows] + both[rows:] + dot(value_high, low)


def kernel(
    n_tm,
    n_space,
    near,
    panels_hbm,
    blocks_hbm,
    mask_ref,
    mixing_ref,
    forward_hbm,
    adjoint_hbm,
    raw,
    first,
    second,
    edge_low,
    edge_high,
    halo_low,
    halo_high,
    band,
    beside,
    turned,
    operator_high,
    operator_low,
    strip_in,
    wide,
    source_low,
    source_high,
    state,
    gram_near,
    gram_far,
    sums,
    combined_ref,
    size_ref,
    scale_ref,
    result,
    local_sem,
    halo_send,
    halo_recv,
    beside_send,
    beside_recv,
    strip_send,
    strip_recv,
    wide_send,
    wide_recv,
    source_send,
    source_recv,
    near_send,
    near_recv,
    far_send,
    far_recv,
    sums_send,
    sums_recv,
):
    a = lax.axis_index("tm")
    s = lax.axis_index("space")
    far = n_space // near
    top = n_tm - 1
    last = 2 * n_tm - 1 - a
    near_base = (s // near) * near
    near_own = s % near
    far_own = s // near
    box_total = n_space * TILE
    has_left = s > 0
    has_right = s < n_space - 1
    always = a >= 0

    barrier = pltpu.get_barrier_semaphore()

    def greet(condition, row, tile):
        @pl.when(condition)
        def _():
            pl.semaphore_signal(barrier, inc=1, device_id=(row, tile), device_id_type=MESH)

        return jnp.where(condition, 1, 0)

    greeted = jnp.int32(near - 1 + far - 1 + n_tm - 1)
    for offset in range(1, near):
        tile = near_base + lax.rem(near_own + offset, near)
        pl.semaphore_signal(barrier, inc=1, device_id=(a, tile), device_id_type=MESH)
    for offset in range(1, far):
        tile = near_own + near * lax.rem(far_own + offset, far)
        pl.semaphore_signal(barrier, inc=1, device_id=(a, tile), device_id_type=MESH)
    for offset in range(1, n_tm):
        row = lax.rem(a + offset, n_tm)
        pl.semaphore_signal(barrier, inc=1, device_id=(row, s), device_id_type=MESH)
    for row_step in (-2, -1, 0, 1, 2):
        for tile_step in (-1, 1):
            row, tile = a + row_step, s + tile_step
            inside = (row >= 0) & (row <= top) & (tile >= 0) & (tile < n_space)
            greeted = greeted + greet(inside, row, tile)

    copy_blocks = pltpu.make_async_copy(blocks_hbm, raw, local_sem.at[0])
    copy_blocks.start()
    copy_panels = pltpu.make_async_copy(
        panels_hbm, wide.at[0, :, pl.ds(EDGE, TILE)], local_sem.at[1]
    )

    @pl.when(a == 0)
    def _():
        copy_panels.start()

    sent = []

    def send(condition, copy):
        sent.append((condition, copy))

        @pl.when(condition)
        def _():
            copy.start()

    def receive(condition, copy):
        @pl.when(condition)
        def _():
            copy.wait_recv()

    def remote(source, target, send_sem, recv_sem, row, tile):
        return pltpu.make_async_remote_copy(
            src_ref=source,
            dst_ref=target,
            send_sem=send_sem,
            recv_sem=recv_sem,
            device_id=(row, tile),
            device_id_type=MESH,
        )

    first[...] = jnp.zeros_like(first)
    second[...] = jnp.zeros_like(second)
    scale_ref[...] = jnp.ones_like(scale_ref)
    scale_ref[0] = jnp.full((8, 128), START, F32)
    size_ref[...] = jnp.full((8, 128), 1.0 / START, F32)
    rows_eye = lax.broadcasted_iota(jnp.int32, (ROWS, 128), 0)
    cols_eye = lax.broadcasted_iota(jnp.int32, (ROWS, 128), 1)
    combined_ref[...] = jnp.where(rows_eye == cols_eye, 1.0, 0.0)

    @pl.when(s == 0)
    def _():
        for pass_index in range(2):
            wide[pass_index, :, 0:EDGE] = jnp.zeros((ROWS, EDGE), F32)
        halo_low[...] = jnp.zeros_like(halo_low)
        beside[0] = jnp.zeros((EDGE, EDGE), F32)

    @pl.when(s == n_space - 1)
    def _():
        for pass_index in range(2):
            wide[pass_index, :, EDGE + TILE : 2 * EDGE + TILE] = jnp.zeros((ROWS, EDGE), F32)
        halo_high[...] = jnp.zeros_like(halo_high)
        beside[1] = jnp.zeros((EDGE, EDGE), F32)

    lane = lax.broadcasted_iota(jnp.int32, (32, 128), 1)
    is_left = lane < BLOCK

    def pair(left, right):
        if left is None:
            even = jnp.where(is_left, 0.0, pltpu.roll(right, BLOCK, 1))
            odd = jnp.where(is_left, 0.0, right)
        elif right is None:
            even = jnp.where(is_left, left, 0.0)
            odd = jnp.where(is_left, pltpu.roll(left, BLOCK, 1), 0.0)
        else:
            even = jnp.where(is_left, left, pltpu.roll(right, BLOCK, 1))
            odd = jnp.where(is_left, pltpu.roll(left, BLOCK, 1), right)
        return even, odd

    def put(target, row, values):
        for parity in range(2):
            target[pl.ds(row + parity, 32, stride=2), :] = values[parity]

    def lanes(ref, start, stop, row, rows):
        tiles = [ref[tile, row : row + rows, :] for tile in range(start, stop)]
        return jnp.concatenate(tiles, axis=1)

    copy_blocks.wait()
    for step in range(2):
        for block in range(TILE_BLOCKS):
            packed = []
            for j in range(3):
                start = (step * 3 + j) * 256 + block
                scale = mask_ref[j, step, block].astype(F32)
                packed.append(raw[pl.ds(start, 32, stride=8), :] * scale)
            if block % 2 == 0:
                tiles = [(None, packed[0]), (packed[1], packed[2])]
                tile_index = block // 2 - 1
            else:
                tiles = [(packed[0], packed[1]), (packed[2], None)]
                tile_index = (block - 1) // 2
            for extra in range(2):
                values = pair(*tiles[extra])
                index = tile_index + extra
                if step == 0:
                    put(first.at[index + 1], block * BLOCK, values)
                elif index < 0:
                    put(edge_low, 0, values)
                elif index >= TILE // 128:
                    put(edge_high, 0, values)
                else:
                    put(second.at[index], block * BLOCK, values)

    pl.semaphore_wait(barrier, greeted)

    def copies_direct(source, row, base):
        right = remote(
            source.at[:, pl.ds(TILE - EDGE, EDGE)],
            wide.at[0, :, pl.ds(0, EDGE)],
            wide_send.at[base],
            wide_recv.at[2],
            row,
            s + 1,
        )
        left = remote(
            source.at[:, pl.ds(0, EDGE)],
            wide.at[0, :, pl.ds(EDGE + TILE, EDGE)],
            wide_send.at[base + 1],
            wide_recv.at[3],
            row,
            s - 1,
        )
        return right, left

    panel_right, panel_left = copies_direct(panels_hbm, a, 2)
    state_right, state_left = copies_direct(state.at[0], a + 1, 4)
    send(has_right & (a == 0), panel_right)
    send(has_left & (a == 0), panel_left)
    halo_right = remote(
        first.at[pl.ds(4, 2), pl.ds(TILE - BLOCK, BLOCK)],
        halo_low,
        halo_send.at[0],
        halo_recv.at[0],
        a,
        s + 1,
    )
    halo_left = remote(
        first.at[pl.ds(0, 2), pl.ds(0, BLOCK)],
        halo_high,
        halo_send.at[1],
        halo_recv.at[1],
        a,
        s - 1,
    )
    send(has_right, halo_right)
    send(has_left, halo_left)

    def formed(group):
        mid = 128 * group
        left = lanes(second, group, group + 3, 256 * group, 256)
        right = lanes(first, 2 * group, 2 * group + 4, mid, 384)
        right_high, right_low = halves(right)
        return product(left, right_high, right_low)

    group_low = formed(0)
    group_high = formed(1)

    row_index = lax.broadcasted_iota(jnp.int32, (ROWS, ROWS), 0)
    col_index = lax.broadcasted_iota(jnp.int32, (ROWS, ROWS), 1)
    same_panel = row_index // COLS == col_index // COLS
    eye = jnp.where(row_index == col_index, 1.0, 0.0).astype(F32)
    spread_rows = lax.broadcasted_iota(jnp.int32, (COLS, ROWS), 0)
    spread_cols = lax.broadcasted_iota(jnp.int32, (COLS, ROWS), 1)
    repeat = jnp.where(spread_cols % COLS == spread_rows, 1.0, 0.0).astype(F32)
    panel_wide = rows_eye // COLS == cols_eye // COLS

    def mixer(step):
        stacked = jnp.concatenate([mixing_ref[step, p] for p in range(PANELS)], axis=0)
        return eye - jnp.where(same_panel, dot_exact(stacked, repeat), 0.0)

    def compact(value):
        padded = jnp.concatenate([value, jnp.zeros((ROWS, 128 - ROWS), F32)], axis=1)
        kept = jnp.where(panel_wide, padded, 0.0)
        total = kept[0:COLS]
        for p in range(1, PANELS):
            total = total + kept[p * COLS : (p + 1) * COLS]
        return total

    def expand(value):
        return jnp.where(panel_wide, jnp.concatenate([value] * PANELS, axis=0), 0.0)

    mixer_first = mixer(0)
    mixer_second = mixer(1)
    sums[a, COLS : 2 * COLS] = compact(dot_exact_nt(eye, dot_exact(mixer_first, mixer_second)))
    sums[last, COLS : 2 * COLS] = compact(dot_exact_nt(eye, dot_exact(mixer_second, mixer_first)))

    receive(has_left, halo_right)
    receive(has_right, halo_left)

    beside_high, beside_low = halves(lanes(halo_low, 0, 2, 0, BLOCK))
    add_low = product(pltpu.roll(edge_low[...], BLOCK, 1)[:, :BLOCK], beside_high, beside_low)
    beside_high, beside_low = halves(lanes(halo_high, 0, 2, 0, BLOCK))
    add_high = product(edge_high[...][:, :BLOCK], beside_high, beside_low)
    band[0] = group_low
    band[1] = group_high
    band[0, 0:BLOCK, 0:256] = group_low[:BLOCK, :256] + add_low
    band[1, 256 - BLOCK : 256, 256:512] = group_high[256 - BLOCK :, 256:] + add_high

    for group in range(2):
        value = jnp.transpose(band[group])
        turned[0, group] = value
        operator_high[0, group], operator_low[0, group] = halves(value)

    beside_right = remote(
        band.at[1, pl.ds(EDGE, EDGE), pl.ds(384, EDGE)],
        beside.at[0],
        beside_send.at[0],
        beside_recv.at[0],
        a,
        s + 1,
    )
    beside_left = remote(
        band.at[0, pl.ds(0, EDGE), pl.ds(0, EDGE)],
        beside.at[1],
        beside_send.at[1],
        beside_recv.at[1],
        a,
        s - 1,
    )

    def copies_strip(source_pass, row, target_pass):
        right = remote(
            turned.at[source_pass, 1, pl.ds(EDGE, STRIP), pl.ds(EDGE, EDGE)],
            strip_in.at[target_pass, 0],
            strip_send.at[source_pass, 0],
            strip_recv.at[target_pass, 0],
            row,
            s + 1,
        )
        left = remote(
            turned.at[source_pass, 0, pl.ds(0, STRIP), pl.ds(0, EDGE)],
            strip_in.at[target_pass, 1],
            strip_send.at[source_pass, 1],
            strip_recv.at[target_pass, 1],
            row,
            s - 1,
        )
        return right, left

    def send_operator():
        strip_right, strip_left = copies_strip(
            0, jnp.minimum(a + 1, top), jnp.where(a < top, 0, 1)
        )
        send((a > 0) & has_right, strip_right)
        send((a > 0) & has_left, strip_left)
        send(has_right, beside_right)
        send(has_left, beside_left)

    strip_adjoint_right, strip_adjoint_left = copies_strip(1, a - 1, 1)

    def prepare_adjoint():
        receive(has_left, beside_right)
        receive(has_right, beside_left)
        blank = jnp.zeros((EDGE, EDGE), F32)
        turned[1, 0, 0:EDGE] = jnp.concatenate([beside[0], blank], axis=1)
        turned[1, 0, EDGE : EDGE + 256] = band[0, :, EDGE : EDGE + 256]
        turned[1, 0, 384:512] = jnp.concatenate([blank, band[1, 0:EDGE, 0:EDGE]], axis=1)
        turned[1, 1, 0:EDGE] = jnp.concatenate([band[0, EDGE : 2 * EDGE, 384:512], blank], axis=1)
        turned[1, 1, EDGE : EDGE + 256] = band[1, :, EDGE : EDGE + 256]
        turned[1, 1, 384:512] = jnp.concatenate([blank, beside[1]], axis=1)
        for group in range(2):
            operator_high[1, group], operator_low[1, group] = halves(turned[1, group])

        @pl.when((a > 0) & has_right)
        def _():
            strip_adjoint_right.start()

        @pl.when((a > 0) & has_left)
        def _():
            strip_adjoint_left.start()

    sent.append(((a > 0) & has_right, strip_adjoint_right))
    sent.append(((a > 0) & has_left, strip_adjoint_left))

    def near_copy(pass_index, offset):
        tile = near_base + lax.rem(near_own + offset, near)
        slot = gram_near.at[pass_index, near_own]
        return remote(
            slot,
            slot,
            near_send.at[pass_index, offset],
            near_recv.at[pass_index, near - offset],
            a,
            tile,
        )

    def far_copy(pass_index, offset):
        tile = near_own + near * lax.rem(far_own + offset, far)
        slot = gram_far.at[pass_index, far_own]
        return remote(
            slot,
            slot,
            far_send.at[pass_index, offset],
            far_recv.at[pass_index, far - offset],
            a,
            tile,
        )

    def sums_copy(pass_index, position, offset):
        row = lax.rem(a + offset, n_tm)
        slot = sums.at[position]
        return remote(
            slot, slot, sums_send.at[pass_index, offset], sums_recv.at[position], row, s
        )

    def start_sums(pass_index):
        value = state[pass_index]
        gram_near[pass_index, near_own] = compact(dot_exact_nt(value, value))
        for offset in range(1, near):
            near_copy(pass_index, offset).start()

    def reduce_near(pass_index):
        for offset in range(1, near):
            near_copy(pass_index, near - offset).wait_recv()
        total = gram_near[pass_index, 0]
        for slot in range(1, near):
            total = total + gram_near[pass_index, slot]
        gram_far[pass_index, far_own] = total
        for offset in range(1, far):
            far_copy(pass_index, offset).start()

    def reduce_far(pass_index, position):
        for offset in range(1, far):
            far_copy(pass_index, far - offset).wait_recv()
        total = gram_far[pass_index, 0]
        for slot in range(1, far):
            total = total + gram_far[pass_index, slot]
        sums[position, 0:COLS] = total
        for offset in range(1, n_tm):
            if pass_index == 0:
                sums_copy(0, position, offset).start()
            else:

                @pl.when(lax.rem(a + offset, n_tm) < a)
                def _():
                    sums_copy(1, position, offset).start()

    out_forward = pltpu.make_async_copy(result.at[0], forward_hbm.at[0], local_sem.at[2])
    out_adjoint = pltpu.make_async_copy(result.at[1], adjoint_hbm.at[0], local_sem.at[3])

    def combine(position, carry):
        @pl.when((position != a) & (position != last))
        def _():
            sums_copy(0, position, 1).wait_recv()

        gram = expand(sums[position, 0:COLS]) / box_total
        mix = expand(sums[position, COLS : 2 * COLS])
        size = jnp.sum(jnp.where(rows_eye == cols_eye, gram, 0.0)) / ROWS
        size = jnp.sqrt(jnp.full((8, 128), size, F32))
        size_before = size_ref[...]
        scale = scale_ref[position]
        mixed = dot_exact(mix[:, :ROWS], combined_ref[...]) / scale[0:1, :]
        squares = jnp.sum(dot_exact(mixed[:, :ROWS], gram) * mixed, axis=1, keepdims=True)
        combined = mixed / jnp.sqrt(jnp.maximum(squares, 0.0) + 1e-06)
        combined_ref[...] = combined
        size_ref[...] = size
        usable = (size > 1e-30) & (size_before > 1e-30)
        ratio = scale * (size_before / jnp.where(usable, size, 1.0))
        scale_ref[position + LAG] = jnp.where(usable, jnp.clip(ratio, 1e-12, 1e12), 1.0)

        @pl.when(position == a)
        def _():
            result[0] = dot_exact(combined[:, :ROWS], state[0])
            out_forward.start()

        @pl.when(position == last)
        def _():
            result[1] = dot_exact(combined[:, :ROWS], state[1])
            out_adjoint.start()

        return carry

    def combine_range(start, stop):
        lax.fori_loop(start, stop, combine, 0)

    def copies_source(pass_index, row, target_pass):
        value = state.at[pass_index]
        base = 4 * pass_index
        return (
            remote(
                value.at[:, pl.ds(TILE - 2 * EDGE, 2 * EDGE)],
                source_low.at[target_pass, :, pl.ds(0, 2 * EDGE)],
                source_send.at[base],
                source_recv.at[target_pass, 0],
                row,
                s + 1,
            ),
            remote(
                value.at[:, pl.ds(0, 2 * EDGE)],
                source_high.at[target_pass, :, pl.ds(EDGE, 2 * EDGE)],
                source_send.at[base + 1],
                source_recv.at[target_pass, 1],
                row,
                s - 1,
            ),
            remote(
                value.at[:, pl.ds(0, EDGE)],
                source_low.at[target_pass, :, pl.ds(2 * EDGE, EDGE)],
                source_send.at[base + 2],
                source_recv.at[target_pass, 2],
                row,
                s,
            ),
            remote(
                value.at[:, pl.ds(TILE - EDGE, EDGE)],
                source_high.at[target_pass, :, pl.ds(0, EDGE)],
                source_send.at[base + 3],
                source_recv.at[target_pass, 3],
                row,
                s,
            ),
        )

    def copy_center(pass_index, row):
        return remote(
            state.at[pass_index],
            wide.at[pass_index, :, pl.ds(EDGE, TILE)],
            wide_send.at[pass_index],
            wide_recv.at[pass_index],
            row,
            s,
        )

    def strips(pass_index, position):
        right, left, own_low, own_high = copies_source(0, a, pass_index)
        strip_right, strip_left = copies_strip(0, a, pass_index)
        scale = scale_ref[position - 1, 0:1, 0:1]
        own_low.wait_recv()
        own_high.wait_recv()

        @pl.when(has_left)
        def _():
            strip_right.wait_recv()
            high, low = halves(strip_in[pass_index, 0])
            right.wait_recv()
            wide[pass_index, :, 0:EDGE] = product(source_low[pass_index], high, low) * scale

        @pl.when(has_right)
        def _():
            strip_left.wait_recv()
            high, low = halves(strip_in[pass_index, 1])
            left.wait_recv()
            wide[pass_index, :, EDGE + TILE : 2 * EDGE + TILE] = (
                product(source_high[pass_index], high, low) * scale
            )

    def apply(pass_index, position):
        scale = scale_ref[position, 0:1, 0:1]
        for group in range(2):
            value = wide[pass_index, :, 256 * group : 256 * group + 512]
            moved = product(
                value, operator_high[pass_index, group], operator_low[pass_index, group]
            )
            state[pass_index, :, 256 * group : 256 * group + 256] = moved * scale

    adjoint_center = copy_center(1, a - 1)
    adjoint_sources = copies_source(1, a - 2, 1)

    def adjoint_position():
        strips(1, last)

        @pl.when(a < top)
        def _():
            adjoint_center.wait_recv()

        apply(1, last)

        @pl.when(a > 0)
        def _():
            adjoint_center.start()

        for copy, condition in zip(adjoint_sources, (has_right, has_left, always, always)):

            @pl.when((a > 1) & condition)
            def _():
                copy.start()

        start_sums(1)

    sent.append((a > 0, adjoint_center))
    for copy, condition in zip(adjoint_sources, (has_right, has_left, always, always)):
        sent.append(((a > 1) & condition, copy))

    send_operator()

    @pl.when(a >= top // 2)
    def _():
        prepare_adjoint()

    before_forward = jnp.maximum(a - LAG + 1, 0)
    combine_range(0, before_forward)

    @pl.when(a == 0)
    def _():
        copy_panels.wait()

    @pl.when(a < 2)
    def _():
        @pl.when(has_left)
        def _():
            state_right.wait_recv()

        @pl.when(has_right)
        def _():
            state_left.wait_recv()

    @pl.when(a >= 2)
    def _():
        strips(0, a)

    forward_center = copy_center(0, a + 1)
    receive(a > 0, forward_center)
    apply(0, a)
    send(a < top, forward_center)
    send((a == 0) & has_right, state_right)
    send((a == 0) & has_left, state_left)
    second_next = jnp.where(a < top - 1, a + 2, jnp.where(a == top - 1, top, top - 1))
    forward_sources = copies_source(0, second_next, jnp.where(a < top - 1, 0, 1))
    for copy, condition in zip(forward_sources, (has_right, has_left, always, always)):
        send(condition, copy)
    start_sums(0)

    @pl.when(a < top // 2)
    def _():
        prepare_adjoint()

    before_adjoint = jnp.maximum(last - LAG + 1, before_forward)

    @pl.when(a == top)
    def _():
        wide[1, :, EDGE : EDGE + TILE] = state[0]
        combine_range(before_forward, before_adjoint)
        adjoint_position()

    reduce_near(0)
    reduce_far(0, a)

    @pl.when(a < top)
    def _():
        combine_range(before_forward, before_adjoint)
        adjoint_position()

    reduce_near(1)
    reduce_far(1, last)
    combine_range(before_adjoint, last + 1)

    for condition, copy in sent:

        @pl.when(condition)
        def _():
            copy.wait_send()

    for pass_index in range(2):
        for offset in range(1, near):
            near_copy(pass_index, offset).wait_send()
        for offset in range(1, far):
            far_copy(pass_index, offset).wait_send()
    for offset in range(1, n_tm):
        sums_copy(0, a, offset).wait_send()

        @pl.when(lax.rem(a + offset, n_tm) < a)
        def _():
            sums_copy(1, last, offset).wait_send()

    out_forward.wait()
    out_adjoint.wait()


def solution(mesh):
    n_tm = mesh.shape["tm"]
    n_space = mesh.shape["space"]
    near = 8 if n_space >= 8 else 2
    far = n_space // near

    def shards(panels_in, blocks, block_mask, mixing):
        lines = blocks.reshape(2, TILE_BLOCKS, 3, 32, 128).transpose(0, 2, 3, 1, 4)
        lines = lines.reshape(2 * 3 * 32 * TILE_BLOCKS, 128)
        dma = pltpu.SemaphoreType.DMA
        vmem = pltpu.VMEM
        scratch = [
            vmem((2 * 3 * 32 * TILE_BLOCKS, 128), F32),
            vmem((6, TILE, 128), F32),
            vmem((4, TILE, 128), F32),
            vmem((BLOCK, 128), F32),
            vmem((BLOCK, 128), F32),
            vmem((2, BLOCK, 128), F32),
            vmem((2, BLOCK, 128), F32),
            vmem((2, 256, 512), F32),
            vmem((2, EDGE, EDGE), F32),
            vmem((2, 2, 512, 256), F32),
            vmem((2, 2, 512, 256), BF16),
            vmem((2, 2, 512, 256), BF16),
            vmem((2, 2, STRIP, EDGE), F32),
            vmem((2, ROWS, TILE + 2 * EDGE), F32),
            vmem((2, ROWS, STRIP), F32),
            vmem((2, ROWS, STRIP), F32),
            vmem((2, ROWS, TILE), F32),
            vmem((2, near, 8, 128), F32),
            vmem((2, far, 8, 128), F32),
            vmem((2 * n_tm, 2 * COLS, 128), F32),
            vmem((ROWS, 128), F32),
            vmem((8, 128), F32),
            vmem((2 * n_tm + LAG, 8, 128), F32),
            vmem((2, ROWS, TILE), F32),
            dma((4,)),
            dma((2,)),
            dma((2,)),
            dma((2,)),
            dma((2,)),
            dma((2, 2)),
            dma((2, 2)),
            dma((6,)),
            dma((4,)),
            dma((8,)),
            dma((2, 4)),
            dma((2, near)),
            dma((2, near)),
            dma((2, far)),
            dma((2, far)),
            dma((2, n_tm)),
            dma((2 * n_tm,)),
        ]
        shape = jax.ShapeDtypeStruct((1, ROWS, TILE), F32)
        return pl.pallas_call(
            functools.partial(kernel, n_tm, n_space, near),
            out_shape=(shape, shape),
            in_specs=[
                pl.BlockSpec(memory_space=pl.ANY),
                pl.BlockSpec(memory_space=pl.ANY),
                pl.BlockSpec(memory_space=pltpu.SMEM),
                pl.BlockSpec(memory_space=pltpu.VMEM),
            ],
            out_specs=(pl.BlockSpec(memory_space=pl.ANY), pl.BlockSpec(memory_space=pl.ANY)),
            scratch_shapes=scratch,
            compiler_params=pltpu.CompilerParams(collective_id=0, has_side_effects=True),
        )(panels_in, lines, block_mask.transpose(2, 0, 1), mixing)

    return jax.shard_map(
        shards,
        mesh=mesh,
        in_specs=(
            P(None, "space"),
            P("tm", "space", None, None),
            P("tm", "space", None),
            P("tm", None, None, None),
        ),
        out_specs=(P("tm", None, "space"), P("tm", None, "space")),
        check_vma=False,
    )
```

time: 1840 us -> 98.9 us (0.05)
  the two profiles are of different devices: /device:TPU:162 before, /device:TPU:8 now
where the time goes in v2:
time: 98.9 us; the launch traced here: 97.3 us
  Pallas kernels  94.5 us (96%)
  local copies, waits for them, and re-layouts  2.14 us (2%)
    pallas_call x1, Pallas kernels, shards(): pl.pallas_call(functools.partial(kernel, n_tm, n_space, near), out_shape=...  94.5 us
    unnamed x4, local copies, waits for them, and re-layouts  2.14 us

profile of v2, /device:TPU:8, one launch (start us, length us, event | category | flops | bytes accessed | tf_op | source)
XLA Modules:
  0.0 97.3 jit_solution(8650172575716390930)
XLA Ops:
  0.6 94.5 %shard_map.59 = (f32[1,32,512]{2,1,0:T(8,128)}, f32[1,32,512]{2,1,0:T(8,128)}) custom-call(f32[32,512]{1,0:T(8,128)} %panels_hbm.1, f32[1536,128]{1,0:T(8,128)} %bitcast.6, s32[3,2,8]{2,1,0:T(2,128)} %bitcast.7, f32[2,4,8,8]{3,2,1,0:T(8,128)} %mixing_ref.1), custom_call_target="tpu_custom_call" | custom-call | tf_op jit(solution)/shard_map/pallas_call | solution.py:769
  95.2 0.0 copy-start
  95.2 1.5 %copy.8 = f32[1,32,512]{2,1,0:T(8,128)} copy(f32[1,32,512]{2,1,0:T(8,128)} %get-tuple-element.4) | data formatting | bytes 131072
  96.7 0.0 copy-done
  96.7 0.6 copy.9
Async XLA Ops:
  95.2 1.5 %copy-start = (f32[1,32,512]{2,1,0:T(8,128)S(1)}, f32[1,32,512]{2,1,0:T(8,128)}, u32[]{:S(2)}) copy-start(f32[1,32,512]{2,1,0:T(8,128)} %get-tuple-element.5) | copy-start | bytes 196612
